TPU v7x, 512 devices: a whole 4x8x8 slice. The times are simulated.
512 devices in a mesh: gx: 16 (over y, z_hi), gy: 32 (over x, z_lo, core).
Axes of the slice: x: 4, y: 8, z: 8 (z_hi: 2, z_lo: 4; z = z_hi * 4 + z_lo), core: 2. Of those that a mesh axis runs over, the one named last changes fastest.
Arguments:
- e_field: float32 [3, 8, 2048, 2048], P(None, None, 'gy', 'gx'), may hold values from -7 to 7
- h_field: float32 [3, 8, 2048, 2048], P(None, None, 'gy', 'gx'), may hold values from -7 to 7
- material: int32 [8, 2048, 2048], P(None, 'gy', 'gx'), may hold values from 0 to 7
- permittivity: float32 [8], replicated, may hold values from 1 to 12
- conductivity: float32 [8], replicated, may hold values from 0.01 to 2
- wire_layers: int32 [8], replicated, may hold values from 0 to 1, as said below
Outputs:
- e_next: float32 [3, 8, 2048, 2048], P(None, None, 'gy', 'gx')
- h_next: float32 [3, 8, 2048, 2048], P(None, None, 'gy', 'gx')
Inputs may be any that keep to these rules, and one draw needn't show every extreme that they name: `wire_layers`: exactly 4 entries are 1.
All inputs are finite; a program needn't handle non-finite values.
Results may differ from a plain program's by a relative error of at most 0.0004.
The roundings to bfloat16 on the way count: a program that leaves them out, or rounds other values in their place, can miss the bound.
Values may be sent and summed in bfloat16 or wider, within the bound.
A program may use at most 128 MiB of HBM per device.

v0:
```python
import math
import jax
import jax.numpy as jnp
from jax import lax
from jax.sharding import PartitionSpec as P

TIME_STEP = 0.9


def shifted(value, axis, steps):
    count = lax.axis_size(axis)
    pairs = [(source, (source + steps) % count) for source in range(count)]
    return lax.ppermute(value, axis, pairs)


def passed_along(shard, axis, by):
    devices = lax.axis_size(axis)
    pairs = [(i, i + by) for i in range(devices) if 0 <= i + by < devices]
    return lax.ppermute(shard, axis, pairs)


def filter_rows(first_idx, n_rows, n_cols):
    row_pos = first_idx + jnp.arange(n_rows, dtype=jnp.int32)
    col_pos = jnp.arange(n_cols, dtype=jnp.int32)
    delta = row_pos[:, None] - col_pos[None, :]
    modes = 2 * (n_cols // 4) + 1
    turned = jnp.mod(modes * delta, 2 * n_cols)
    safe_delta = jnp.where(delta == 0, 1, delta)
    upper = jnp.sin(math.pi * turned.astype(jnp.float32) / n_cols)
    lower = n_cols * jnp.sin(math.pi * safe_delta.astype(jnp.float32) / n_cols)
    band = jnp.where(delta == 0, modes / n_cols, upper / lower)
    return (0.7 * band + jnp.where(delta == 0, 0.3, 0.0)).astype(jnp.bfloat16)


def face_x(planes, direction):
    return shifted(planes, "gx", direction)


def face_y(planes, direction):
    return passed_along(planes, "gy", direction)


def ahead_z(comp):
    zeros = jnp.zeros_like(comp[:1])
    return jnp.concatenate([comp[1:], zeros], axis=0) - comp


def behind_z(comp):
    zeros = jnp.zeros_like(comp[:1])
    return comp - jnp.concatenate([zeros, comp[:-1]], axis=0)


def ahead_x(comp, edge_col):
    return jnp.concatenate([comp[:, :, 1:], edge_col[:, :, None]], axis=2) - comp


def behind_x(comp, edge_col):
    return comp - jnp.concatenate([edge_col[:, :, None], comp[:, :, :-1]], axis=2)


def ahead_y(comp, edge_row):
    return jnp.concatenate([comp[:, 1:, :], edge_row[:, None, :]], axis=1) - comp


def behind_y(comp, edge_row):
    return comp - jnp.concatenate([edge_row[:, None, :], comp[:, :-1, :]], axis=1)


def curl_of_e(e_field):
    next_x = face_x(e_field[1:3, :, :, 0], -1)
    next_y = face_y(jnp.stack([e_field[0, :, 0, :], e_field[2, :, 0, :]]), -1)
    e_x, e_y, e_z = (e_field[0], e_field[1], e_field[2])
    curl_x = ahead_y(e_z, next_y[1]) - ahead_z(e_y)
    curl_y = ahead_z(e_x) - ahead_x(e_z, next_x[1])
    curl_z = ahead_x(e_y, next_x[0]) - ahead_y(e_x, next_y[0])
    return jnp.stack([curl_x, curl_y, curl_z])


def curl_of_h(h_field):
    last_col = h_field.shape[3] - 1
    last_row = h_field.shape[2] - 1
    prev_x = face_x(h_field[1:3, :, :, last_col], 1)
    prev_y = face_y(jnp.stack([h_field[0, :, last_row, :], h_field[2, :, last_row, :]]), 1)
    h_x, h_y, h_z = (h_field[0], h_field[1], h_field[2])
    curl_x = behind_y(h_z, prev_y[1]) - behind_z(h_y)
    curl_y = behind_z(h_x) - behind_x(h_z, prev_x[1])
    curl_z = behind_x(h_y, prev_x[0]) - behind_y(h_x, prev_y[0])
    return jnp.stack([curl_x, curl_y, curl_z])


def smooth(field_in, wire_layers):
    block_rows = field_in.shape[2]
    n_layers = field_in.shape[1]
    n_wires = n_layers // 2
    n_lines = block_rows * lax.axis_size("gy")
    rank = jnp.cumsum(wire_layers) - 1
    slots = jnp.arange(n_wires, dtype=jnp.int32)
    picked = (wire_layers[None] == 1) & (rank[None] == slots[:, None])
    layer_of = jnp.sum(jnp.where(picked, jnp.arange(n_layers, dtype=jnp.int32)[None], 0), axis=1)
    wires = jnp.concatenate(
        [lax.dynamic_slice_in_dim(field_in, layer_of[k], 1, axis=1) for k in range(n_wires)], axis=1
    )
    rounded = wires.astype(jnp.bfloat16)
    f_rows = filter_rows(lax.axis_index("gy") * block_rows, block_rows, n_lines)
    filtered = jnp.einsum(
        "mn,cznx->czmx",
        f_rows,
        lax.all_gather(rounded, "gy", axis=2, tiled=True),
        preferred_element_type=jnp.float32,
    )
    out = field_in
    for k in range(n_wires):
        out = lax.dynamic_update_slice_in_dim(out, filtered[:, k : k + 1], layer_of[k], axis=1)
    return out


def body(e_field, h_field, material, permittivity, conductivity, wire_layers):
    h_half = h_field - TIME_STEP * curl_of_e(e_field)
    h_next = smooth(h_half, wire_layers)
    ratio_tab = conductivity * TIME_STEP / (2.0 * permittivity)
    decay_tab = (1.0 - ratio_tab) / (1.0 + ratio_tab)
    gain_tab = TIME_STEP / permittivity / (1.0 + ratio_tab)
    labels = jnp.arange(permittivity.shape[0], dtype=jnp.int32)
    onehot = (material[None] == labels[:, None, None, None]).astype(jnp.float32)
    decay = jnp.sum(onehot * decay_tab[:, None, None, None], axis=0)
    gain = jnp.sum(onehot * gain_tab[:, None, None, None], axis=0)
    e_half = decay[None] * e_field + gain[None] * curl_of_h(h_next)
    e_next = smooth(e_half, wire_layers)
    return (e_next, h_next)


def solution(mesh):
    placed = (
        P(None, None, "gy", "gx"),
        P(None, None, "gy", "gx"),
        P(None, "gy", "gx"),
        P(),
        P(),
        P(),
    )
    return jax.shard_map(
        body,
        mesh=mesh,
        in_specs=placed,
        out_specs=(P(None, None, "gy", "gx"), P(None, None, "gy", "gx")),
        check_vma=False,
    )
```

profile of v0, /device:TPU:1, one launch (start us, length us, event | category | flops | bytes accessed | tf_op | source)
XLA Modules:
  0.0 211.4 jit_solution(1662647163732602079)
XLA Ops:
  7.2 0.0 copy-start.1
  7.2 0.0 copy-start.3
  7.2 0.0 all-gather.3.cloned.1.call-start
  7.2 0.9 fusion.58
  8.1 8.7 %collective-permute-start = (f32[2,8,128]{2,1,0:T(8,128)S(1)}, f32[2,8,128]{2,1,0:T(8,128)S(1)}, u32[]{:S(2)}, u32[]{:S(2)}) collective-permute-start(f32[2,8,128]{2,1,0:T(8,128)S(1)} %pad_maximum_fusion.2), channel_id=1, source_target_pairs={{1,0},{2,1},{3,2},{4,3},{5,4},{6,5},{7,6},{8,7},{9,8},{10,9},{11,1... | collective-permute-start | bytes 24584 | tf_op jit(solution)/shard_map/ppermute | solution.py:19
  16.9 1.1 slice.172
  18.0 0.2 copy.62
  18.2 0.0 copy-start.4
  18.2 8.3 %collective-permute-start.1 = (f32[2,8,64]{2,1,0:T(8,128)S(1)}, f32[2,8,64]{2,1,0:T(8,128)S(1)}, u32[]{:S(2)}, u32[]{:S(2)}) collective-permute-start(f32[2,8,64]{2,1,0:T(8,128)S(1)} %bitcast.112), channel_id=1, source_target_pairs={{0,480},{32,0},{64,32},{96,64},{128,96},{160,128},{192,160},{224,1... | collective-permute-start | bytes 12296 | tf_op jit(solution)/shard_map/ppermute | solution.py:13
  26.5 1.1 slice_bitcast_fusion.13
  27.6 1.1 slice_bitcast_fusion.8
  28.7 0.7 broadcast_compare_fusion
  29.3 0.8 reduce-window.8
  30.2 0.1 slice_bitcast_fusion.4
  30.3 0.1 select_reduce_fusion.2
  30.4 0.6 fusion.61
  38.7 0.0 collective-permute-done.1
  38.7 0.1 copy.52
  38.9 0.2 copy.53
  39.0 0.0 collective-permute-done
  39.1 1.3 slice_bitcast_fusion.5
  40.3 0.1 slice.210
  40.5 0.2 fusion.17
  40.8 0.1 fusion
  40.9 0.7 pad_maximum_fusion
  41.6 0.0 all-gather.3.cloned.1.call-update
  41.7 0.0 all-gather.5.cloned.1.call-start
  41.8 0.4 select_reduce_fusion.1
  42.2 64.1 %all-gather.3.cloned.1.call-done = bf16[3,4,2048,128]{3,2,1,0:T(8,128)(2,1)} async-done(((bf16[3,4,64,128]{3,2,1,0:T(8,128)(2,1)}), bf16[3,4,2048,128]{3,2,1,0:T(8,128)(2,1)}) %all-gather.3.cloned.1.call-update) | async-done | bytes 6291472 | tf_op jit(solution)/shard_map/all_gather | solution.py:108
  106.3 6.9 %convolution_bitcast_fusion.1 = f32[3,4,64,128]{3,2,1,0:T(8,128)S(1)} fusion(bf16[3,4,2048,128]{3,2,1,0:T(8,128)(2,1)} %all-gather.3.cloned.1.call-done, s32[64]{0:T(128)S(1)} %iota_add_fusion), kind=kOutput, calls=%fused_computation.4 | convolution fusion | flops 406061056 | bytes 6684928 | tf_op jit(solution)/shard_map/mn,cznx->czmx/dot_general | solution.py:105
  113.2 0.0 copy-start
  113.3 0.4 slice_reduce_fusion
  113.7 0.7 slice_bitcast_fusion.11
  114.4 3.2 %collective-permute-start.2 = (f32[2,8,128]{2,1,0:T(8,128)S(1)}, f32[2,8,128]{2,1,0:T(8,128)S(1)}, u32[]{:S(2)}, u32[]{:S(2)}) collective-permute-start(f32[2,8,128]{2,1,0:T(8,128)S(1)} %pad_maximum_fusion.3), channel_id=1, source_target_pairs={{0,1},{1,2},{2,3},{3,4},{4,5},{5,6},{6,7},{7,8},{8,9},{9,10},{10,1... | collective-permute-start | bytes 24584 | tf_op jit(solution)/shard_map/ppermute | solution.py:19
  117.6 5.7 %collective-permute-start.3 = (f32[2,8,64]{2,1,0:T(8,128)S(1)}, f32[2,8,64]{2,1,0:T(8,128)S(1)}, u32[]{:S(2)}, u32[]{:S(2)}) collective-permute-start(f32[2,8,64]{2,1,0:T(8,128)S(1)} %slice_reduce_fusion), channel_id=1, source_target_pairs={{0,32},{32,64},{64,96},{96,128},{128,160},{160,192},{192,224},{224... | collective-permute-start | bytes 12296 | tf_op jit(solution)/shard_map/ppermute | solution.py:13
  123.4 4.7 %collective-permute-done.3 = f32[2,8,64]{2,1,0:T(8,128)S(1)} collective-permute-done((f32[2,8,64]{2,1,0:T(8,128)S(1)}, f32[2,8,64]{2,1,0:T(8,128)S(1)}, u32[]{:S(2)}, u32[]{:S(2)}) %collective-permute-start.3) | collective-permute-done | bytes 4128 | tf_op jit(solution)/shard_map/ppermute | solution.py:13
  128.0 0.2 copy.57
  128.2 0.2 copy.58
  128.4 0.0 collective-permute-done.2
  128.4 0.2 slice_bitcast_fusion.2
  128.6 1.1 fusion.22
  129.7 0.2 fusion.1
  129.9 0.7 pad_maximum_fusion.1
  130.6 0.0 all-gather.5.cloned.1.call-update
  130.6 66.0 %all-gather.5.cloned.1.call-done = bf16[3,4,2048,128]{3,2,1,0:T(8,128)(2,1)} async-done(((bf16[3,4,64,128]{3,2,1,0:T(8,128)(2,1)}), bf16[3,4,2048,128]{3,2,1,0:T(8,128)(2,1)}) %all-gather.5.cloned.1.call-update) | async-done | bytes 6291472 | tf_op jit(solution)/shard_map/all_gather | solution.py:108
  196.7 6.9 %convolution_bitcast_fusion = f32[3,4,64,128]{3,2,1,0:T(8,128)S(1)} fusion(bf16[3,4,2048,128]{3,2,1,0:T(8,128)(2,1)} %all-gather.5.cloned.1.call-done, s32[64]{0:T(128)S(1)} %iota_add_fusion), kind=kOutput, calls=%fused_computation.3 | convolution fusion | flops 406061056 | bytes 6684928 | tf_op jit(solution)/shard_map/mn,cznx->czmx/dot_general | solution.py:105
  203.6 0.0 copy-start.2
  203.6 0.9 copy-done.2
  (34 shorter events, 0.4 us)
Async XLA Ops:
  7.2 33.3 %copy-start.1 = (f32[3,8,64,128]{3,2,1,0:T(8,128)S(1)}, f32[3,8,64,128]{3,2,1,0:T(8,128)}, u32[]{:S(2)}) copy-start(f32[3,8,64,128]{3,2,1,0:T(8,128)} %param.6) | copy-start | bytes 2359300
  7.2 33.6 %copy-start.3 = (f32[3,8,64,128]{3,2,1,0:T(8,128)S(1)}, f32[3,8,64,128]{3,2,1,0:T(8,128)}, u32[]{:S(2)}) copy-start(f32[3,8,64,128]{3,2,1,0:T(8,128)} %param.7) | copy-start | bytes 2359300
  7.2 99.1 %all-gather.3.cloned.1.call-start = ((), (), s32[]{:S(2)}) async-start(), calls=%async_computation | async-start | bytes 6488064 | tf_op jit(solution)/shard_map/all_gather | solution.py:108
  8.1 30.9 %collective-permute-start = (f32[2,8,128]{2,1,0:T(8,128)S(1)}, f32[2,8,128]{2,1,0:T(8,128)S(1)}, u32[]{:S(2)}, u32[]{:S(2)}) collective-permute-start(f32[2,8,128]{2,1,0:T(8,128)S(1)} %pad_maximum_fusion.2), channel_id=1, source_target_pairs={{1,0},{2,1},{3,2},{4,3},{5,4},{6,5},{7,6},{8,7},{9,8},{10,9},{11,1... | collective-permute-start | bytes 24584 | tf_op jit(solution)/shard_map/ppermute | solution.py:19
  18.2 23.6 %copy-start.5 = (f32[8]{0:T(128)S(1)}, f32[8]{0:T(128)}, u32[]{:S(2)}) copy-start(f32[8]{0:T(128)} %param.9) | copy-start | bytes 100
  18.2 23.6 %copy-start.6 = (f32[8]{0:T(128)S(1)}, f32[8]{0:T(128)}, u32[]{:S(2)}) copy-start(f32[8]{0:T(128)} %param.10) | copy-start | bytes 100
  18.2 23.6 %copy-start.4 = (s32[8,64,128]{2,1,0:T(8,128)S(1)}, s32[8,64,128]{2,1,0:T(8,128)}, u32[]{:S(2)}) copy-start(s32[8,64,128]{2,1,0:T(8,128)} %param.8) | copy-start | bytes 786436
  18.2 20.5 %collective-permute-start.1 = (f32[2,8,64]{2,1,0:T(8,128)S(1)}, f32[2,8,64]{2,1,0:T(8,128)S(1)}, u32[]{:S(2)}, u32[]{:S(2)}) collective-permute-start(f32[2,8,64]{2,1,0:T(8,128)S(1)} %bitcast.112), channel_id=1, source_target_pairs={{0,480},{32,0},{64,32},{96,64},{128,96},{160,128},{192,160},{224,1... | collective-permute-start | bytes 12296 | tf_op jit(solution)/shard_map/ppermute | solution.py:13
  41.7 155.0 %all-gather.5.cloned.1.call-start = ((), (), s32[]{:S(2)}) async-start(), calls=%async_computation.1 | async-start | bytes 6488064 | tf_op jit(solution)/shard_map/all_gather | solution.py:108
  113.2 17.4 %copy-start = (f32[3,8,64,128]{3,2,1,0:T(8,128)}, f32[3,8,64,128]{3,2,1,0:T(8,128)S(1)}, u32[]{:S(2)}) copy-start(f32[3,8,64,128]{3,2,1,0:T(8,128)S(1)} %slice_dynamic-update-slice_fusion.4) | copy-start | bytes 2359300
  114.4 13.9 %collective-permute-start.2 = (f32[2,8,128]{2,1,0:T(8,128)S(1)}, f32[2,8,128]{2,1,0:T(8,128)S(1)}, u32[]{:S(2)}, u32[]{:S(2)}) collective-permute-start(f32[2,8,128]{2,1,0:T(8,128)S(1)} %pad_maximum_fusion.3), channel_id=1, source_target_pairs={{0,1},{1,2},{2,3},{3,4},{4,5},{5,6},{6,7},{7,8},{8,9},{9,10},{10,1... | collective-permute-start | bytes 24584 | tf_op jit(solution)/shard_map/ppermute | solution.py:19
  117.6 10.4 %collective-permute-start.3 = (f32[2,8,64]{2,1,0:T(8,128)S(1)}, f32[2,8,64]{2,1,0:T(8,128)S(1)}, u32[]{:S(2)}, u32[]{:S(2)}) collective-permute-start(f32[2,8,64]{2,1,0:T(8,128)S(1)} %slice_reduce_fusion), channel_id=1, source_target_pairs={{0,32},{32,64},{64,96},{96,128},{128,160},{160,192},{192,224},{224... | collective-permute-start | bytes 12296 | tf_op jit(solution)/shard_map/ppermute | solution.py:13
  203.6 0.9 copy-start.2
Sparse Core Ops, SparseCore 0:
  41.8 64.4 all-gather.2
  130.8 65.8 all-gather.4
where the time goes:
time: 212 us; the launch traced here: 211 us
  waiting for transfers between devices  135 us (64%)
  starting transfers between devices  26 us (12%)
  between operations  22.1 us (10%)
  matrix products  13.7 us (6%)
  local copies, waits for them, and re-layouts  8.13 us (4%)
  other arithmetic  6.55 us (3%)
    all_gather x2, waiting for transfers between devices, smooth(): lax.all_gather(rounded, 'gy', axis=2, tiled=True)  130 us
    ppermute x2, starting transfers between devices, shifted(): return lax.ppermute(value, axis, pairs)  14 us
    dot_general x2, matrix products, smooth(): jnp.einsum('mn,cznx->czmx', f_rows, lax.all_gather(rounded, 'gy', axis=2,...  13.7 us
    ppermute x2, starting transfers between devices, passed_along(): return lax.ppermute(shard, axis, pairs)  11.9 us
    ppermute x2, waiting for transfers between devices, shifted(): return lax.ppermute(value, axis, pairs)  4.69 us
  transfers between devices with their start and end apart: 6, of which 3 were waited for; matrix products, arithmetic and copies ran while one was open for 3% of the time, Pallas kernels for 0%

commit v1 on v0

--- a/solution.py
+++ b/solution.py
@@ -105,7 +105,9 @@
     filtered = jnp.einsum(
         "mn,cznx->czmx",
         f_rows,
-        lax.all_gather(rounded, "gy", axis=2, tiled=True),
+        jnp.concatenate(
+            lax.all_to_all(jnp.stack([rounded] * lax.axis_size("gy")), "gy", 0, 0), axis=2
+        ),
         preferred_element_type=jnp.float32,
     )
     out = field_in

time: 212 us -> 388 us (1.83)
  waiting for transfers between devices: 135 us -> 284 us
  local copies, waits for them, and re-layouts: 8.13 us -> 43.3 us
  between operations: 22.1 us -> 8.78 us
  starting transfers between devices: 26 us -> 36.6 us
  matrix products: 13.7 us -> 9.4 us
    all_to_all x0 -> x2, waiting for transfers between devices: none -> 277 us  [smooth(): lax.all_to_all(jnp.stack([rounded] * lax.axis_size('gy')), 'gy', 0, 0)]
    all_gather x2 -> x0, waiting for transfers between devices: 130 us -> none  [smooth(): lax.all_gather(rounded, 'gy', axis=2, tiled=True)]
    dynamic_update_slice x8, local copies, waits for them, and re-layouts: 0.11 us -> 15.5 us  [smooth(): lax.dynamic_update_slice_in_dim(out, filtered[:, k:k + 1], layer_of[k], a...]
    all_to_all x0 -> x2, starting transfers between devices: none -> 15.3 us  [smooth(): lax.all_to_all(jnp.stack([rounded] * lax.axis_size('gy')), 'gy', 0, 0)]
    another operation x2 -> x8, local copies, waits for them, and re-layouts: 0.08 us -> 9.16 us  [the longest x2 8.41 us: smooth(): jnp.stack([rounded] * lax.axis_size('gy'))]
    reshape x0 -> x2, local copies, waits for them, and re-layouts: none -> 8.56 us  [smooth(): jnp.concatenate(lax.all_to_all(jnp.stack([rounded] * lax.axis_size('gy'))...]
    ppermute x2, starting transfers between devices: 11.9 us -> 4.78 us  [passed_along(): return lax.ppermute(shard, axis, pairs)]
    dot_general x2, matrix products: 13.7 us -> 9.4 us  [smooth(): jnp.einsum('mn,cznx->czmx', f_rows, jnp.concatenate(lax.all_to_all(jnp.st...]
  transfers between devices with their start and end apart: 6 -> 6, of which waited for: 3 -> 3; matrix products, arithmetic and copies ran while one was open for 3% -> 2% of each run, Pallas kernels for 0% -> 0%
where the time goes in v1:
time: 388 us; the launch traced here: 387 us
  waiting for transfers between devices  284 us (73%)
  local copies, waits for them, and re-layouts  43.3 us (11%)
  starting transfers between devices  36.6 us (9%)
  matrix products  9.4 us (2%)
  between operations  8.78 us (2%)
  other arithmetic  5.63 us (1%)
    all_to_all x2, waiting for transfers between devices, smooth(): lax.all_to_all(jnp.stack([rounded] * lax.axis_size('gy')), 'gy', 0, 0)  277 us
    ppermute x2, starting transfers between devices, shifted(): return lax.ppermute(value, axis, pairs)  16.5 us
    dynamic_update_slice x8, local copies, waits for them, and re-layouts, smooth(): lax.dynamic_update_slice_in_dim(out, filtered[:, k:k + 1], layer_of[k], a...  15.5 us
    all_to_all x2, starting transfers between devices, smooth(): lax.all_to_all(jnp.stack([rounded] * lax.axis_size('gy')), 'gy', 0, 0)  15.3 us
    dot_general x2, matrix products, smooth(): jnp.einsum('mn,cznx->czmx', f_rows, jnp.concatenate(lax.all_to_all(jnp.st...  9.4 us
    reshape x2, local copies, waits for them, and re-layouts, smooth(): jnp.concatenate(lax.all_to_all(jnp.stack([rounded] * lax.axis_size('gy'))...  8.56 us
    another operation x2, local copies, waits for them, and re-layouts, smooth(): jnp.stack([rounded] * lax.axis_size('gy'))  8.41 us
  transfers between devices with their start and end apart: 6, of which 3 were waited for; matrix products, arithmetic and copies ran while one was open for 2% of the time, Pallas kernels for 0%

profile of v1, /device:TPU:1, one launch (start us, length us, event | category | flops | bytes accessed | tf_op | source)
XLA Modules:
  0.0 387.2 jit_solution(17449883475078725413)
XLA Ops:
  0.6 1.2 slice.172
  1.8 0.2 copy.231
  2.0 14.4 %collective-permute-start.1 = (f32[2,8,64]{2,1,0:T(8,128)S(1)}, f32[2,8,64]{2,1,0:T(8,128)S(1)}, u32[]{:S(2)}, u32[]{:S(2)}) collective-permute-start(f32[2,8,64]{2,1,0:T(8,128)S(1)} %bitcast.121), channel_id=1, source_target_pairs={{0,480},{32,0},{64,32},{96,64},{128,96},{160,128},{192,160},{224,1... | collective-permute-start | bytes 12296 | tf_op jit(solution)/shard_map/ppermute | solution.py:13
  16.4 1.6 copy.200
  18.0 2.9 collective-permute-start
  21.0 0.7 broadcast_compare_fusion
  21.6 0.8 reduce-window.8
  22.7 0.7 fusion.59
  31.1 0.2 copy.210
  31.2 0.2 copy.211
  31.8 0.2 fusion.17
  32.0 0.5 fusion
  32.5 0.4 dynamic-slice_convert_fusion.7
  32.9 0.5 pad_maximum_fusion
  33.4 4.2 %stack.24 = bf16[32,3,4,64,128]{4,3,2,1,0:T(8,128)(2,1)} broadcast(bf16[3,4,64,128]{3,2,1,0:T(8,128)(2,1)S(1)} %copy.213), dimensions={1,2,3,4} | broadcast | bytes 6488064 | tf_op jit(solution)/shard_map/stack | solution.py:109
  37.6 7.5 %all-to-all-start = ((bf16[32,3,4,64,128]{4,3,2,1,0:T(8,128)(2,1)}), bf16[32,3,4,64,128]{4,3,2,1,0:T(8,128)(2,1)}, u32[]{:S(2)}, u32[]{:S(2)}) async-start(bf16[32,3,4,64,128]{4,3,2,1,0:T(8,128)(2,1)} %stack.24), calls=%async_computation | async-start | bytes 12582912 | tf_op jit(solution)/shard_map/all_to_all | solution.py:109
  45.1 0.4 select_reduce_fusion.1
  45.9 138.6 %all-to-all-done = bf16[32,3,4,64,128]{4,3,2,1,0:T(8,128)(2,1)} async-done(((bf16[32,3,4,64,128]{4,3,2,1,0:T(8,128)(2,1)}), bf16[32,3,4,64,128]{4,3,2,1,0:T(8,128)(2,1)}, u32[]{:S(2)}, u32[]{:S(2)}) %all-to-all-start) | async-done | bytes 6291488 | tf_op jit(solution)/shard_map/all_to_all | solution.py:109
  184.5 4.3 %copy.214 = bf16[3,4,32,64,128]{4,3,2,1,0:T(8,128)(2,1)S(1)} copy(bf16[3,4,32,64,128]{4,3,1,0,2:T(8,128)(2,1)} %bitcast.22) | data formatting | bytes 12582912 | tf_op jit(solution)/shard_map/reshape | solution.py:108
  188.8 4.7 %convolution_bitcast_fusion.1 = f32[3,4,64,128]{3,2,1,0:T(8,128)S(1)} fusion(bf16[3,4,2048,128]{3,2,1,0:T(8,128)(2,1)S(1)} %bitcast.111, s32[64]{0:T(128)S(1)} %iota_add_fusion), kind=kOutput, calls=%fused_computation.4 | convolution fusion | flops 406061056 | bytes 6684928 | tf_op jit(solution)/shard_map/mn,cznx->czmx/dot_general | solution.py:105
  193.5 1.9 dynamic_update_slice.24
  195.5 1.9 dynamic_update_slice.25
  197.4 1.9 dynamic_update_slice.26
  199.3 1.9 dynamic_update_slice.27
  201.3 0.2 slice.236
  201.5 0.7 slice_bitcast_fusion.10
  202.3 1.9 collective-permute-start.2
  204.2 0.2 copy.219
  204.4 2.1 collective-permute-start.3
  206.6 1.7 slice_bitcast_fusion.8
  208.3 6.6 %collective-permute-done.3 = f32[2,8,64]{2,1,0:T(8,128)S(1)} collective-permute-done((f32[2,8,64]{2,1,0:T(8,128)S(1)}, f32[2,8,64]{2,1,0:T(8,128)S(1)}, u32[]{:S(2)}, u32[]{:S(2)}) %collective-permute-start.3) | collective-permute-done | bytes 4128 | tf_op jit(solution)/shard_map/ppermute | solution.py:13
  214.9 0.2 copy.220
  215.0 0.2 copy.221
  215.2 1.1 slice_bitcast_fusion.3
  216.5 0.5 fusion.1
  217.1 0.4 dynamic-slice_convert_fusion.3
  217.5 0.5 pad_maximum_fusion.1
  218.0 4.2 %stack.29 = bf16[32,3,4,64,128]{4,3,2,1,0:T(8,128)(2,1)} broadcast(bf16[3,4,64,128]{3,2,1,0:T(8,128)(2,1)S(1)} %copy.222), dimensions={1,2,3,4} | broadcast | bytes 6488064 | tf_op jit(solution)/shard_map/stack | solution.py:109
  222.2 7.8 %all-to-all-start.1 = ((bf16[32,3,4,64,128]{4,3,2,1,0:T(8,128)(2,1)}), bf16[32,3,4,64,128]{4,3,2,1,0:T(8,128)(2,1)}, u32[]{:S(2)}, u32[]{:S(2)}) async-start(bf16[32,3,4,64,128]{4,3,2,1,0:T(8,128)(2,1)} %stack.29), calls=%async_computation.1 | async-start | bytes 12582912 | tf_op jit(solution)/shard_map/all_to_all | solution.py:109
  230.0 1.0 copy.229
  231.0 138.4 %all-to-all-done.1 = bf16[32,3,4,64,128]{4,3,2,1,0:T(8,128)(2,1)} async-done(((bf16[32,3,4,64,128]{4,3,2,1,0:T(8,128)(2,1)}), bf16[32,3,4,64,128]{4,3,2,1,0:T(8,128)(2,1)}, u32[]{:S(2)}, u32[]{:S(2)}) %all-to-all-start.1) | async-done | bytes 6291488 | tf_op jit(solution)/shard_map/all_to_all | solution.py:109
  369.4 4.3 %copy.223 = bf16[3,4,32,64,128]{4,3,2,1,0:T(8,128)(2,1)S(1)} copy(bf16[3,4,32,64,128]{4,3,1,0,2:T(8,128)(2,1)} %bitcast.47) | data formatting | bytes 12582912 | tf_op jit(solution)/shard_map/reshape | solution.py:108
  373.7 4.7 %convolution_bitcast_fusion = f32[3,4,64,128]{3,2,1,0:T(8,128)S(1)} fusion(bf16[3,4,2048,128]{3,2,1,0:T(8,128)(2,1)S(1)} %bitcast.110, s32[64]{0:T(128)S(1)} %iota_add_fusion), kind=kOutput, calls=%fused_computation.3 | convolution fusion | flops 406061056 | bytes 6684928 | tf_op jit(solution)/shard_map/mn,cznx->czmx/dot_general | solution.py:105
  378.4 1.9 dynamic_update_slice.28
  380.3 1.9 dynamic_update_slice.29
  382.3 1.9 dynamic_update_slice.30
  384.2 1.9 dynamic_update_slice.31
  386.2 1.0 copy.228
  (43 shorter events, 1.4 us)
Async XLA Ops:
  0.6 31.3 %copy-start.1 = (f32[3,8,64,128]{3,2,1,0:T(8,128)S(1)}, f32[3,8,64,128]{3,2,1,0:T(8,128)}, u32[]{:S(2)}) copy-start(f32[3,8,64,128]{3,2,1,0:T(8,128)} %param.7) | copy-start | bytes 2359300
  2.0 29.0 %collective-permute-start.1 = (f32[2,8,64]{2,1,0:T(8,128)S(1)}, f32[2,8,64]{2,1,0:T(8,128)S(1)}, u32[]{:S(2)}, u32[]{:S(2)}) collective-permute-start(f32[2,8,64]{2,1,0:T(8,128)S(1)} %bitcast.121), channel_id=1, source_target_pairs={{0,480},{32,0},{64,32},{96,64},{128,96},{160,128},{192,160},{224,1... | collective-permute-start | bytes 12296 | tf_op jit(solution)/shard_map/ppermute | solution.py:13
  18.0 13.4 %collective-permute-start = (f32[2,8,128]{2,1,0:T(8,128)S(1)}, f32[2,8,128]{2,1,0:T(8,128)S(1)}, u32[]{:S(2)}, u32[]{:S(2)}) collective-permute-start(f32[2,8,128]{2,1,0:T(8,128)S(1)} %pad_maximum_fusion.2), channel_id=1, source_target_pairs={{1,0},{2,1},{3,2},{4,3},{5,4},{6,5},{7,6},{8,7},{9,8},{10,9},{11,1... | collective-permute-start | bytes 24584 | tf_op jit(solution)/shard_map/ppermute | solution.py:19
  37.6 7.5 %copy-start.3 = (f32[8]{0:T(128)S(1)}, f32[8]{0:T(128)}, u32[]{:S(2)}) copy-start(f32[8]{0:T(128)} %param.9) | copy-start | bytes 100
  37.6 7.5 %copy-start.4 = (f32[8]{0:T(128)S(1)}, f32[8]{0:T(128)}, u32[]{:S(2)}) copy-start(f32[8]{0:T(128)} %param.10) | copy-start | bytes 100
  37.6 7.6 %copy-start.2 = (s32[8,64,128]{2,1,0:T(8,128)S(1)}, s32[8,64,128]{2,1,0:T(8,128)}, u32[]{:S(2)}) copy-start(s32[8,64,128]{2,1,0:T(8,128)} %param.8) | copy-start | bytes 786436
  37.6 146.9 %all-to-all-start = ((bf16[32,3,4,64,128]{4,3,2,1,0:T(8,128)(2,1)}), bf16[32,3,4,64,128]{4,3,2,1,0:T(8,128)(2,1)}, u32[]{:S(2)}, u32[]{:S(2)}) async-start(bf16[32,3,4,64,128]{4,3,2,1,0:T(8,128)(2,1)} %stack.24), calls=%async_computation | async-start | bytes 12582912 | tf_op jit(solution)/shard_map/all_to_all | solution.py:109
  193.5 23.1 %copy-start = (f32[3,8,64,128]{3,2,1,0:T(8,128)S(1)}, f32[3,8,64,128]{3,2,1,0:T(8,128)}, u32[]{:S(2)}) copy-start(f32[3,8,64,128]{3,2,1,0:T(8,128)} %param.6) | copy-start | bytes 2359300
  202.3 12.9 %collective-permute-start.2 = (f32[2,8,128]{2,1,0:T(8,128)S(1)}, f32[2,8,128]{2,1,0:T(8,128)S(1)}, u32[]{:S(2)}, u32[]{:S(2)}) collective-permute-start(f32[2,8,128]{2,1,0:T(8,128)S(1)} %pad_maximum_fusion.3), channel_id=1, source_target_pairs={{0,1},{1,2},{2,3},{3,4},{4,5},{5,6},{6,7},{7,8},{8,9},{9,10},{10,1... | collective-permute-start | bytes 24584 | tf_op jit(solution)/shard_map/ppermute | solution.py:19
  204.4 10.4 %collective-permute-start.3 = (f32[2,8,64]{2,1,0:T(8,128)S(1)}, f32[2,8,64]{2,1,0:T(8,128)S(1)}, u32[]{:S(2)}, u32[]{:S(2)}) collective-permute-start(f32[2,8,64]{2,1,0:T(8,128)S(1)} %bitcast.122), channel_id=1, source_target_pairs={{0,32},{32,64},{64,96},{96,128},{128,160},{160,192},{192,224},{224... | collective-permute-start | bytes 12296 | tf_op jit(solution)/shard_map/ppermute | solution.py:13
  222.2 147.2 %all-to-all-start.1 = ((bf16[32,3,4,64,128]{4,3,2,1,0:T(8,128)(2,1)}), bf16[32,3,4,64,128]{4,3,2,1,0:T(8,128)(2,1)}, u32[]{:S(2)}, u32[]{:S(2)}) async-start(bf16[32,3,4,64,128]{4,3,2,1,0:T(8,128)(2,1)} %stack.29), calls=%async_computation.1 | async-start | bytes 12582912 | tf_op jit(solution)/shard_map/all_to_all | solution.py:109
